TPU v7x, 256 devices: a whole 4x4x8 slice. The times are simulated.
256 devices in a mesh: ctxa: 32 (over x, z), ctxb: 8 (over y, core).
Axes of the slice: x: 4, y: 4, z: 8, core: 2. Of those that a mesh axis runs over, the one named last changes fastest.
Arguments:
- tokens: bfloat16 [32768, 1024], P(('ctxa', 'ctxb')), may hold values from -80 to 80
- w_query: bfloat16 [1024, 512], replicated, may hold values from -0.1875 to 0.1875
- w_key: bfloat16 [1024, 512], replicated, may hold values from -0.1875 to 0.1875
- w_value: bfloat16 [1024, 512], replicated, may hold values from -0.1875 to 0.1875
- w_slot: bfloat16 [8, 64, 128], replicated, may hold values from -3 to 3
- w_out: bfloat16 [512, 1024], replicated, may hold values from -1 to 1
Outputs:
- mixed: bfloat16 [32768, 1024], P(('ctxa', 'ctxb'))
All inputs are finite; a program needn't handle non-finite values.
Results may differ from a plain program's by a relative error of at most 0.012.
The roundings to bfloat16 on the way count: a program that leaves them out, or rounds other values in their place, can miss the bound.
Values may be sent and summed in bfloat16 or wider, within the bound.
A program may use at most 192 MiB of HBM per device.

v0:
```python
import jax
import jax.numpy as jnp
from jax import lax
from jax.sharding import PartitionSpec as P

HEADS = 8
HEAD_DIM = 64
SLOTS = 128
WINDOW = 128


def padded_2(block, sides, width):
    for axis, dim in sides:
        count = lax.axis_size(axis)
        forward = [(i, i + 1) for i in range(count - 1)]
        backward = [(target, source) for source, target in forward]
        low = lax.ppermute(
            lax.slice_in_dim(block, block.shape[dim] - width, None, axis=dim), axis, forward
        )
        high = lax.ppermute(lax.slice_in_dim(block, 0, width, axis=dim), axis, backward)
        block = jnp.concatenate([low, block, high], axis=dim)
    return block


def layer_norm(values):
    center = values - jnp.mean(values, axis=-1, keepdims=True)
    spread = jnp.mean(center * center, axis=-1, keepdims=True)
    return center * lax.rsqrt(spread + 1e-05)


def finish_slots(total, sums):
    slot_keys = layer_norm(sums[..., :HEAD_DIM]).astype(jnp.bfloat16)
    slot_values = (sums[..., HEAD_DIM:] / total[..., None]).astype(jnp.bfloat16)
    return (slot_keys, slot_values)


def per_device(tokens, w_query, w_key, w_value, w_slot, w_out):
    rows = tokens.shape[0]
    width = HEADS * HEAD_DIM
    query = jnp.dot(tokens, w_query, preferred_element_type=jnp.float32).astype(jnp.bfloat16)
    key = jnp.dot(tokens, w_key, preferred_element_type=jnp.float32).astype(jnp.bfloat16)
    value = jnp.dot(tokens, w_value, preferred_element_type=jnp.float32).astype(jnp.bfloat16)
    key_heads = key.reshape(rows, HEADS, HEAD_DIM)
    logits = jnp.einsum("thd,hds->hts", key_heads, w_slot, preferred_element_type=jnp.float32)
    paired = jnp.concatenate([key_heads, value.reshape(rows, HEADS, HEAD_DIM)], axis=2).astype(
        jnp.float32
    )
    local_top = jnp.max(logits, axis=1)
    top = lax.pmax(local_top, ("ctxa", "ctxb"))
    weight = jnp.exp(logits - top[:, None, :])
    total = jnp.sum(weight, axis=1)
    sums = jnp.einsum("hts,thd->hsd", weight, paired, precision=lax.Precision.HIGHEST)
    total, sums = lax.psum((total, sums), ("ctxa", "ctxb"))
    slot_keys, slot_values = finish_slots(total, sums)
    near_keys = layer_norm(key_heads.astype(jnp.float32)).astype(jnp.bfloat16).reshape(rows, width)
    stacked = jnp.concatenate([near_keys, value], axis=1)
    padded = padded_2(stacked, ((("ctxa", "ctxb"), 0),), WINDOW)
    seq_len = rows * lax.axis_size(("ctxa", "ctxb"))
    offset = lax.axis_index(("ctxa", "ctxb")) * rows
    block = min(512, rows)
    span = block + 2 * WINDOW
    scale = 1.0 / HEAD_DIM**0.5
    groups = 2
    group_heads = HEADS // groups
    group_width = group_heads * HEAD_DIM
    grouped_keys = slot_keys.reshape(groups, group_heads, SLOTS, HEAD_DIM)
    grouped_values = slot_values.reshape(groups, group_heads, SLOTS, HEAD_DIM)
    blocks = rows // block

    def attend(item):
        index = item // groups
        group = item % groups
        start = index * block
        column = group * group_width
        query_block = lax.dynamic_slice_in_dim(query, column, group_width, 1).reshape(
            block, group_heads, HEAD_DIM
        )
        keys_block = lax.dynamic_slice_in_dim(padded, column, group_width, 1).reshape(
            span, group_heads, HEAD_DIM
        )
        values_block = lax.dynamic_slice_in_dim(padded, width + column, group_width, 1).reshape(
            span, group_heads, HEAD_DIM
        )
        group_slot_keys = lax.dynamic_index_in_dim(grouped_keys, group, 0, keepdims=False)
        group_slot_values = lax.dynamic_index_in_dim(grouped_values, group, 0, keepdims=False)
        query_pos = offset + start + jnp.arange(block, dtype=jnp.int32)
        key_pos = offset + start - WINDOW + jnp.arange(span, dtype=jnp.int32)
        valid = (
            (jnp.abs(key_pos[None, :] - query_pos[:, None]) <= WINDOW)
            & (key_pos[None, :] >= 0)
            & (key_pos[None, :] < seq_len)
        )
        near = (
            jnp.einsum("bhd,khd->hbk", query_block, keys_block, preferred_element_type=jnp.float32)
            * scale
        )
        near = jnp.where(valid[None], near, -1e30)
        far = (
            jnp.einsum(
                "bhd,hsd->hbs", query_block, group_slot_keys, preferred_element_type=jnp.float32
            )
            * scale
        )
        top_score = jnp.maximum(jnp.max(near, axis=-1), jnp.max(far, axis=-1))
        near_exp = jnp.exp(near - top_score[..., None])
        far_exp = jnp.exp(far - top_score[..., None])
        denom = jnp.sum(near_exp, axis=-1) + jnp.sum(far_exp, axis=-1)
        near_probs = (near_exp / denom[..., None]).astype(jnp.bfloat16)
        far_probs = (far_exp / denom[..., None]).astype(jnp.bfloat16)
        result = jnp.einsum(
            "hbk,khd->bhd", near_probs, values_block, preferred_element_type=jnp.float32
        )
        result = result + jnp.einsum(
            "hbs,hsd->bhd", far_probs, group_slot_values, preferred_element_type=jnp.float32
        )
        return result.reshape(block, group_width).astype(jnp.bfloat16)

    pieces = lax.map(attend, jnp.arange(blocks * groups, dtype=jnp.int32))
    attended = (
        pieces.reshape(blocks, groups, block, group_width)
        .transpose(0, 2, 1, 3)
        .reshape(rows, width)
    )
    return jnp.dot(attended, w_out, preferred_element_type=jnp.float32).astype(jnp.bfloat16)


def solution(mesh):
    in_specs = (P(("ctxa", "ctxb"), None), P(), P(), P(), P(), P())
    out_specs = P(("ctxa", "ctxb"), None)
    return jax.shard_map(
        per_device, mesh=mesh, in_specs=in_specs, out_specs=out_specs, check_vma=False
    )
```

profile of v0, /device:TPU:2, one launch (start us, length us, event | category | flops | bytes accessed | tf_op | source)
XLA Modules:
  0.0 378.1 jit_solution(4458475252980913308)
XLA Ops:
  6.5 1.8 convolution_convert_fusion.3
  9.3 0.7 pad_maximum_fusion.1
  10.0 1.9 collective-permute-start
  11.9 9.6 %collective-permute-start.1 = (bf16[128,1024]{1,0:T(8,128)(2,1)}, bf16[128,1024]{1,0:T(8,128)(2,1)}, u32[]{:S(2)}, u32[]{:S(2)}) collective-permute-start(bf16[128,1024]{1,0:T(8,128)(2,1)} %pad_maximum_fusion.1), channel_id=1, source_target_pairs={{1,0},{2,1},{3,2},{4,3},{5,4},{6,5},{7,6},{8,7},{9,8},{10,9},{11,1... | collective-permute-start | bytes 786440 | tf_op jit(solution)/shard_map/ppermute | solution.py:20
  21.7 0.9 copy.21
  22.8 72.5 %pmax.7 = f32[8,128]{1,0:T(8,128)S(1)} all-reduce(f32[8,128]{1,0:T(8,128)S(1)} %get-tuple-element.154), channel_id=1, replica_groups=mesh['ctxa'=32,'ctxb'=8] {'ctxa','ctxb'}, use_global_device_ids=true, to_apply=%region_3.0 | all-reduce | flops 1024 | bytes 8192 | tf_op jit(solution)/shard_map/pmax | solution.py:49
  95.5 2.5 fusion.17
  98.1 75.0 %psum.15 = f32[8,128]{1,0:T(8,128)S(1)} all-reduce(f32[8,128]{1,0:T(8,128)S(1)} %fusion.16), channel_id=1, replica_groups=mesh['ctxa'=32,'ctxb'=8] {'ctxa','ctxb'}, use_global_device_ids=true, to_apply=%region_8.0 | all-reduce | flops 1024 | bytes 8192 | tf_op jit(solution)/shard_map/psum | solution.py:53
  173.5 179.0 %all-reduce.2.cloned.1.call-done = f32[8,128,128]{2,1,0:T(8,128)} async-done(((f32[8,128,128]{2,1,0:T(8,128)}), f32[8,128,128]{2,1,0:T(8,128)}) %all-reduce.2.cloned.1.call-update) | async-done | bytes 524304 | tf_op jit(solution)/shard_map/psum | solution.py:53
  352.4 1.3 slice_reduce_fusion
  353.8 1.4 multiply_reduce_fusion
  355.2 0.6 fusion.15
  356.1 1.1 pad_maximum_fusion
  357.2 0.4 copy.24
  357.6 11.7 %while.12 = (s32[]{:T(128)}, bf16[2,128,256]{1,2,0:T(8,128)(2,1)}, s32[2]{0:T(128)S(1)}, bf16[384,1024]{0,1:T(8,128)(2,1)S(1)}, s32[]{:T(128)}, /*index=5*/bf16[...) while((s32[]{:T(128)}, bf16[2,128,256]{1,2,0:T(8,128)(2,1)}, ...), condition=%wide.region_14.15_spmd, body=%wide.region_9.14_spmd.sunk | while | flops 69452448 | bytes 5446203 | solution.py:118
  357.6 0.6 dynamic_slice.60
  361.2 0.4 fusion.63
  362.4 0.4 fusion.67
  362.8 0.6 constant_dynamic-update-slice_fusion.2
  363.5 0.6 dynamic_slice.60
  367.1 0.4 fusion.63
  368.3 0.4 fusion.67
  368.7 0.6 constant_dynamic-update-slice_fusion.2
  369.3 1.9 convolution_convert_fusion
  (64 shorter events, 4.4 us)
Async XLA Ops:
  6.5 362.8 %copy-start = (bf16[512,1024]{1,0:T(8,128)(2,1)S(1)}, bf16[512,1024]{1,0:T(8,128)(2,1)}, u32[]{:S(2)}) copy-start(bf16[512,1024]{1,0:T(8,128)(2,1)} %param.13) | copy-start | bytes 3145732
  6.5 1.9 copy-start.2
  6.5 1.9 copy-start.3
  6.5 345.9 %all-reduce.2.cloned.1.call-start = ((), (), s32[]{:S(2)}) async-start(), calls=%async_computation | async-start | bytes 1048576 | tf_op jit(solution)/shard_map/psum | solution.py:53
  9.2 13.3 %copy-start.5 = (bf16[8,64,128]{2,1,0:T(8,128)(2,1)S(1)}, bf16[8,64,128]{2,1,0:T(8,128)(2,1)}, u32[]{:S(2)}) copy-start(bf16[8,64,128]{2,1,0:T(8,128)(2,1)} %param.12) | copy-start | bytes 393220
  10.0 346.1 %collective-permute-start = (bf16[128,1024]{1,0:T(8,128)(2,1)}, bf16[128,1024]{1,0:T(8,128)(2,1)}, u32[]{:S(2)}, u32[]{:S(2)}) collective-permute-start(bf16[128,1024]{1,0:T(8,128)(2,1)} %pad_maximum_fusion.1), channel_id=1, source_target_pairs={{0,1},{1,2},{2,3},{3,4},{4,5},{5,6},{6,7},{7,8},{8,9},{9,10},{10,1... | collective-permute-start | bytes 786440 | tf_op jit(solution)/shard_map/ppermute | solution.py:17
  11.9 344.2 %collective-permute-start.1 = (bf16[128,1024]{1,0:T(8,128)(2,1)}, bf16[128,1024]{1,0:T(8,128)(2,1)}, u32[]{:S(2)}, u32[]{:S(2)}) collective-permute-start(bf16[128,1024]{1,0:T(8,128)(2,1)} %pad_maximum_fusion.1), channel_id=1, source_target_pairs={{1,0},{2,1},{3,2},{4,3},{5,4},{6,5},{7,6},{8,7},{9,8},{10,9},{11,1... | collective-permute-start | bytes 786440 | tf_op jit(solution)/shard_map/ppermute | solution.py:20
  95.5 77.7 %copy-start.4 = (bf16[1024,512]{1,0:T(8,128)(2,1)S(1)}, bf16[1024,512]{1,0:T(8,128)(2,1)}, u32[]{:S(2)}) copy-start(bf16[1024,512]{1,0:T(8,128)(2,1)} %param.9) | copy-start | bytes 3145732
  352.4 2.8 copy-start.1
Sparse Core Ops, SparseCore 0:
  98.2 254.2 all-reduce.1
where the time goes:
time: 379 us; the launch traced here: 378 us
  waiting for transfers between devices  179 us (47%)
  blocking collectives  147 us (39%)
  between operations  13.7 us (4%)
  starting transfers between devices  11.5 us (3%)
  matrix products  9.54 us (3%)
  other arithmetic  6.44 us (2%)
  loops' own time  5.47 us (1%)
  local copies, waits for them, and re-layouts  4.99 us (1%)
    psum x1, waiting for transfers between devices, per_device(): total, sums = lax.psum((total, sums), ('ctxa', 'ctxb'))  179 us
    psum x1, blocking collectives, per_device(): total, sums = lax.psum((total, sums), ('ctxa', 'ctxb'))  75 us
    pmax x1, blocking collectives, per_device(): top = lax.pmax(local_top, ('ctxa', 'ctxb'))  72.5 us
    ppermute x1, starting transfers between devices, padded_2(): lax.ppermute(lax.slice_in_dim(block, 0, width, axis=dim), axis, backward)  9.63 us
  transfers between devices with their start and end apart: 3, of which 1 were waited for; matrix products, arithmetic and copies ran while one was open for 2% of the time, Pallas kernels for 0%

commit v1 on v0

--- a/solution.py
+++ b/solution.py
@@ -50,7 +50,7 @@
     weight = jnp.exp(logits - top[:, None, :])
     total = jnp.sum(weight, axis=1)
     sums = jnp.einsum("hts,thd->hsd", weight, paired, precision=lax.Precision.HIGHEST)
-    total, sums = lax.psum((total, sums), ("ctxa", "ctxb"))
+    total, sums = lax.psum(lax.psum((total, sums), "ctxa"), "ctxb")
     slot_keys, slot_values = finish_slots(total, sums)
     near_keys = layer_norm(key_heads.astype(jnp.float32)).astype(jnp.bfloat16).reshape(rows, width)
     stacked = jnp.concatenate([near_keys, value], axis=1)

time: 379 us -> 347 us (0.916)
  the two profiles are of different devices: /device:TPU:2 before, /device:TPU:1 now
where the time goes in v1:
time: 347 us
  blocking collectives  171 us (49%)
  waiting for transfers between devices  134 us (39%)
  between operations  13.7 us (4%)
  matrix products  8.49 us (2%)
  loops' own time  5.81 us (2%)
  other arithmetic  4.7 us (1%)
  starting transfers between devices  4.51 us (1%)
  local copies, waits for them, and re-layouts  4.48 us (1%)
    psum x2, waiting for transfers between devices, per_device(): total, sums = lax.psum(lax.psum((total, sums), 'ctxa'), 'ctxb')  134 us
    psum x2, blocking collectives, per_device(): total, sums = lax.psum(lax.psum((total, sums), 'ctxa'), 'ctxb')  89.4 us
    pmax x1, blocking collectives, per_device(): top = lax.pmax(local_top, ('ctxa', 'ctxb'))  81.4 us
  transfers between devices with their start and end apart: 4, of which 1 were waited for; matrix products, arithmetic and copies ran while one was open for 0% of the time, Pallas kernels for 0%

profile of v1, /device:TPU:1, one launch (start us, length us, event | category | flops | bytes accessed | tf_op | source)
XLA Modules:
  0.0 346.7 jit_solution(1086859893066846800)
XLA Ops:
  6.5 1.7 convolution_convert_fusion.3
  8.9 81.4 %pmax.7 = f32[8,128]{1,0:T(8,128)S(1)} all-reduce(f32[8,128]{1,0:T(8,128)S(1)} %get-tuple-element.154), channel_id=1, replica_groups=mesh['ctxa'=32,'ctxb'=8] {'ctxa','ctxb'}, use_global_device_ids=true, to_apply=%region_3.0 | all-reduce | flops 1024 | bytes 8192 | tf_op jit(solution)/shard_map/pmax | solution.py:49
  90.3 0.3 convolution_convert_fusion.2
  90.9 1.5 fusion.17
  93.0 2.1 collective-permute-start
  95.1 2.4 collective-permute-start.1
  97.5 0.3 convolution_convert_fusion.1
  97.9 134.1 %all-reduce.3.cloned.1.call-done = f32[8,128,128]{2,1,0:T(8,128)} async-done(((f32[8,128,128]{2,1,0:T(8,128)}), f32[8,128,128]{2,1,0:T(8,128)}) %all-reduce.3.cloned.1.call-update) | async-done | bytes 524304 | tf_op jit(solution)/shard_map/psum | solution.py:53
  232.1 58.4 %psum.30 = f32[8,128]{1,0:T(8,128)S(1)} all-reduce(f32[8,128]{1,0:T(8,128)S(1)} %fusion.16), channel_id=1, replica_groups=mesh['ctxa'=32,'ctxb'=8] {'ctxa'}, use_global_device_ids=true, to_apply=%region_9.0 | all-reduce | flops 1024 | bytes 8192 | tf_op jit(solution)/shard_map/psum | solution.py:53
  290.6 30.9 %psum.31 = f32[8,128]{1,0:T(8,128)S(1)} all-reduce(f32[8,128]{1,0:T(8,128)S(1)} %psum.30), channel_id=1, replica_groups=mesh['ctxa'=32,'ctxb'=8] {'ctxb'}, use_global_device_ids=true, to_apply=%region_10.0 | all-reduce | flops 1024 | bytes 8192 | tf_op jit(solution)/shard_map/psum | solution.py:53
  321.6 0.4 copy.24
  322.0 1.3 slice_reduce_fusion
  323.3 1.4 multiply_reduce_fusion
  324.8 0.6 fusion.15
  325.7 12.2 %while.12 = (s32[]{:T(128)}, bf16[2,128,256]{1,2,0:T(8,128)(2,1)}, s32[2]{0:T(128)S(1)}, bf16[384,1024]{0,1:T(8,128)(2,1)S(1)}, s32[]{:T(128)}, /*index=5*/bf16[...) while((s32[]{:T(128)}, bf16[2,128,256]{1,2,0:T(8,128)(2,1)}, ...), condition=%wide.region_16.17_spmd, body=%wide.region_11.16_spmd.sunk | while | flops 69452448 | bytes 5446203 | solution.py:118
  325.7 0.7 dynamic_slice.60
  329.5 0.4 fusion.63
  330.8 0.4 fusion.67
  331.2 0.6 constant_dynamic-update-slice_fusion.2
  331.8 0.7 dynamic_slice.60
  335.6 0.4 fusion.63
  336.9 0.4 fusion.67
  337.2 0.6 constant_dynamic-update-slice_fusion.2
  337.9 1.9 convolution_convert_fusion
  (68 shorter events, 4.2 us)
Async XLA Ops:
  6.5 331.3 %copy-start = (bf16[512,1024]{1,0:T(8,128)(2,1)S(1)}, bf16[512,1024]{1,0:T(8,128)(2,1)}, u32[]{:S(2)}) copy-start(bf16[512,1024]{1,0:T(8,128)(2,1)} %param.13) | copy-start | bytes 3145732
  6.5 2.1 copy-start.5
  6.5 225.5 %all-reduce.3.cloned.1.call-start = ((), (), s32[]{:S(2)}) async-start(), calls=%async_computation | async-start | bytes 1048576 | tf_op jit(solution)/shard_map/psum | solution.py:53
  8.3 82.0 %copy-start.2 = (bf16[128,1024]{1,0:T(8,128)(2,1)S(1)}, bf16[128,1024]{1,0:T(8,128)(2,1)}, u32[]{:S(2)}) copy-start(bf16[128,1024]{1,0:T(8,128)(2,1)} %param.8) | copy-start | bytes 786436
  8.3 82.0 %copy-start.3 = (bf16[1024,512]{1,0:T(8,128)(2,1)S(1)}, bf16[1024,512]{1,0:T(8,128)(2,1)}, u32[]{:S(2)}) copy-start(bf16[1024,512]{1,0:T(8,128)(2,1)} %param.11) | copy-start | bytes 3145732
  92.5 229.5 %all-reduce.5.cloned.1.call-start = ((), (), s32[]{:S(2)}) async-start(), calls=%async_computation.1 | async-start | bytes 1048576 | tf_op jit(solution)/shard_map/psum | solution.py:53
  92.9 4.6 %copy-start.4 = (bf16[1024,512]{1,0:T(8,128)(2,1)S(1)}, bf16[1024,512]{1,0:T(8,128)(2,1)}, u32[]{:S(2)}) copy-start(bf16[1024,512]{1,0:T(8,128)(2,1)} %param.9) | copy-start | bytes 3145732
  93.0 228.5 %collective-permute-start = (bf16[128,1024]{1,0:T(8,128)(2,1)S(1)}, bf16[128,1024]{1,0:T(8,128)(2,1)S(1)}, u32[]{:S(2)}, u32[]{:S(2)}) collective-permute-start(bf16[128,1024]{1,0:T(8,128)(2,1)S(1)} %pad_maximum_fusion.1), channel_id=1, source_target_pairs={{0,1},{1,2},{2,3},{3,4},{4,5},{5,6},{6,7},{7,8},{8,9},{9,10},{10,1... | collective-permute-start | bytes 786440 | tf_op jit(solution)/shard_map/ppermute | solution.py:17
  95.1 226.4 %collective-permute-start.1 = (bf16[128,1024]{1,0:T(8,128)(2,1)S(1)}, bf16[128,1024]{1,0:T(8,128)(2,1)S(1)}, u32[]{:S(2)}, u32[]{:S(2)}) collective-permute-start(bf16[128,1024]{1,0:T(8,128)(2,1)S(1)} %pad_maximum_fusion.1), channel_id=1, source_target_pairs={{1,0},{2,1},{3,2},{4,3},{5,4},{6,5},{7,6},{8,7},{9,8},{10,9},{11,1... | collective-permute-start | bytes 786440 | tf_op jit(solution)/shard_map/ppermute | solution.py:20
  322.0 2.8 copy-start.1
Sparse Core Ops, SparseCore 0:
  92.6 139.3 all-reduce.2
  234.4 65.6 all-reduce.4
